TPU v7x, 128 devices: a whole 4x4x4 slice. The times are simulated.
128 devices in a mesh: rep: 4 (over z_lo, core), shard: 32 (over y, z_hi, x).
Axes of the slice: x: 4, y: 4, z: 4 (z_hi: 2, z_lo: 2; z = z_hi * 2 + z_lo), core: 2. Of those that a mesh axis runs over, the one named last changes fastest.
Arguments:
- weight: bfloat16 [4, 32, 512, 2048], P('rep', None, 'shard'), may hold values from -3 to 3
- tracker: float32 [4, 32, 512, 2048], P('rep', None, 'shard'), may hold values from -40 to 40, as said below
- grad_new: bfloat16 [4, 32, 512, 2048], P('rep', None, 'shard'), may hold values from -6 to 6
- grad_old: bfloat16 [4, 32, 512, 2048], P('rep', None, 'shard'), may hold values from -6 to 6
- mix_keep: int32 [4, 2], replicated, may hold values from 4 to 12, as said below
Outputs:
- new_weight: bfloat16 [4, 32, 512, 2048], P('rep', None, 'shard')
- new_tracker: float32 [4, 32, 512, 2048], P('rep', None, 'shard')
- update: bfloat16 [4, 32, 512, 2048], P('rep', None, 'shard')
Inputs may be any that keep to these rules, and one draw needn't show every extreme that they name: `mix_keep`: every entry is one of the integers 4 to 12; some entry equals 4 and some equals 12. `tracker`: finite real values.
All inputs are finite; a program needn't handle non-finite values.
Results may differ from a plain program's by a relative error of at most 0.023.
Values may be sent and summed in bfloat16 or wider, within the bound.
A program may use at most 128 MiB of HBM per device.

v0:
```python
import math
import jax
import jax.numpy as jnp
from jax import lax
from jax.sharding import PartitionSpec as P

NS_STEPS = 5
coeff_a = 3.4445
coeff_b = -4.775
coeff_c = 2.0315
learn_rate = 0.05


def swapped(shard, axis, bit):
    return lax.ppermute(shard, axis, [(i, i ^ 1 << bit) for i in range(lax.axis_size(axis))])


def gossip_weight(values, keep_row):
    for bit_index in range(keep_row.shape[0]):
        partner = swapped(values, "rep", bit_index)
        own_share = keep_row[bit_index] / 16.0
        other_share = (16.0 - keep_row[bit_index]) / 16.0
        values = (
            own_share * values.astype(jnp.float32) + other_share * partner.astype(jnp.float32)
        ).astype(jnp.bfloat16)
    return values


def gossip_tracker(values, keep_row):
    for bit_index in range(keep_row.shape[0]):
        partner = swapped(values.astype(jnp.bfloat16), "rep", bit_index).astype(values.dtype)
        own_share = keep_row[bit_index] / 16.0
        other_share = (16.0 - keep_row[bit_index]) / 16.0
        values = own_share * values + other_share * partner
    return values


def orthogonalize(block_in):
    update_scale = 0.2 * math.sqrt(max(block_in.shape[1], block_in.shape[2]))
    values = block_in.astype(jnp.float32)
    frob_norm = jnp.sqrt(jnp.sum(values * values, axis=(1, 2), keepdims=True))
    iterate = (values / (frob_norm + 1e-07)).astype(jnp.bfloat16)
    for iteration in range(NS_STEPS):
        gram_matrix = jnp.einsum(
            "kmn,kpn->kmp", iterate, iterate, preferred_element_type=jnp.float32
        ).astype(jnp.bfloat16)
        square = jnp.einsum(
            "kmp,kpq->kmq", gram_matrix, gram_matrix, preferred_element_type=jnp.float32
        )
        polynomial = (coeff_b * gram_matrix.astype(jnp.float32) + coeff_c * square).astype(
            jnp.bfloat16
        )
        product = jnp.einsum(
            "kmp,kpn->kmn", polynomial, iterate, preferred_element_type=jnp.float32
        )
        iterate = (coeff_a * iterate.astype(jnp.float32) + product).astype(jnp.bfloat16)
    return (update_scale * iterate.astype(jnp.float32)).astype(jnp.bfloat16)


def settle(block_in):
    update_block = orthogonalize(block_in[0])[None]
    return lax.all_to_all(update_block, "shard", split_axis=2, concat_axis=0, tiled=True)


def local(weight, tracker, grad_new, grad_old, mix_keep):
    rep_index = lax.axis_index("rep")
    keep_all = mix_keep.astype(jnp.float32)
    keep_row = keep_all[rep_index]
    mixed_w = gossip_weight(weight, keep_row)
    mixed_y = gossip_tracker(tracker, keep_row)
    new_tracker = mixed_y + grad_new.astype(jnp.float32) - grad_old.astype(jnp.float32)
    rounded = new_tracker.astype(jnp.bfloat16)
    shards = lax.axis_size("shard")
    experts = rounded.shape[1]
    packed = rounded.reshape(shards, experts // shards, rounded.shape[2], rounded.shape[3])
    returned = settle(lax.all_to_all(packed, "shard", split_axis=0, concat_axis=2, tiled=True))
    update = returned.reshape(rounded.shape)
    new_weight = (mixed_w.astype(jnp.float32) - learn_rate * update.astype(jnp.float32)).astype(
        jnp.bfloat16
    )
    return (new_weight, new_tracker, update)


def solution(mesh):
    return jax.shard_map(
        local,
        mesh=mesh,
        in_specs=(
            P("rep", None, "shard", None),
            P("rep", None, "shard", None),
            P("rep", None, "shard", None),
            P("rep", None, "shard", None),
            P(),
        ),
        out_specs=(
            P("rep", None, "shard", None),
            P("rep", None, "shard", None),
            P("rep", None, "shard", None),
        ),
        check_vma=False,
    )
```

profile of v0, /device:TPU:0, one launch (start us, length us, event | category | flops | bytes accessed | tf_op | source)
XLA Modules:
  0.0 211.0 jit_solution(15291772610491671655)
XLA Ops:
  0.6 0.0 copy-start.5
  0.6 3.8 %convert_element_type.215 = bf16[1,32,16,2048]{3,2,1,0:T(8,128)(2,1)} convert(f32[1,32,16,2048]{3,2,1,0:T(8,128)} %param.6) | non-fusion elementwise | flops 1048576 | bytes 6291456 | tf_op jit(solution)/shard_map/convert_element_type | solution.py:31
  4.5 0.0 collective-permute-start.2
  4.5 0.0 copy-done.5
  4.5 0.1 constant_dynamic-slice_fusion
  4.6 0.5 fusion.34
  6.4 2.5 %collective-permute-done.2 = bf16[1,32,16,2048]{3,2,1,0:T(8,128)(2,1)S(1)} collective-permute-done((bf16[1,32,16,2048]{3,2,1,0:T(8,128)(2,1)}, bf16[1,32,16,2048]{3,2,1,0:T(8,128)(2,1)S(1)}, u32[]{:S(2)}, u32[]{:S(2)}) %collective-permute-start.2) | collective-permute-done | bytes 2097184 | tf_op jit(solution)/shard_map/ppermute | solution.py:15
  8.8 0.0 copy-start
  8.8 0.0 copy-start.2
  8.8 0.0 copy-start.3
  8.8 3.1 %fusion.3 = bf16[1,32,16,2048]{3,2,1,0:T(8,128)(2,1)S(1)} fusion(bf16[1,32,16,2048]{3,2,1,0:T(8,128)(2,1)S(1)} %collective-permute-done.2, f32[1,32,16,2048]{3,2,1,0:T(8,128)} %param.6, f32[]{:T(128)} %bitcast.2, f32[]{:T(128)} %bitcast.1), kind=kLoop, calls=%fused_computation.16 | loop fusion | flops 5242880 | bytes 8388616 | tf_op jit(solution)/shard_map/convert_element_type | solution.py:31
  11.9 2.1 collective-permute-start.3
  14.0 0.0 collective-permute-start
  15.3 44.6 %collective-permute-done.3 = bf16[1,32,16,2048]{3,2,1,0:T(8,128)(2,1)S(1)} collective-permute-done((bf16[1,32,16,2048]{3,2,1,0:T(8,128)(2,1)S(1)}, bf16[1,32,16,2048]{3,2,1,0:T(8,128)(2,1)S(1)}, u32[]{:S(2)}, u32[]{:S(2)}) %collective-permute-start.3) | collective-permute-done | bytes 2097184 | tf_op jit(solution)/shard_map/ppermute | solution.py:15
  60.0 0.0 copy-done
  60.0 0.0 copy-done.2
  60.0 0.0 copy-done.3
  60.0 4.9 %convert_bitcast_fusion = (bf16[32,1,16,2048]{3,2,1,0:T(8,128)(2,1)}, f32[1,32,16,2048]{3,2,1,0:T(8,128)}) fusion(bf16[1,32,16,2048]{3,2,1,0:T(8,128)(2,1)S(1)} %copy-done.2, bf16[1,32,16,2048]{3,2,1,0:T(8,128)(2,1)S(1)} %copy-done.3, bf16[1,32,16,2048]{3,2,1,0:T(8,128)(2,1)S(1)} %collective-permute-done.3, f32[]{:T(128)} %bitcast.3, ...), kind=kLoop, calls=%fused_computation.17 | loop fusion | flops 13631488 | bytes 18874384 | tf_op jit(solution)/shard_map/reshape | solution.py:75
  64.9 10.5 %all-to-all-start = ((bf16[32,1,16,2048]{3,2,1,0:T(8,128)(2,1)}), bf16[32,1,16,2048]{3,2,1,0:T(8,128)(2,1)S(1)}, u32[]{:S(2)}, u32[]{:S(2)}) async-start(bf16[32,1,16,2048]{3,2,1,0:T(8,128)(2,1)} %get-tuple-element.3), calls=%async_computation | async-start | bytes 4194304 | tf_op jit(solution)/shard_map/all_to_all | solution.py:76
  75.3 0.0 collective-permute-done
  75.3 4.6 %add_convert_fusion.6 = bf16[1,32,16,2048]{3,2,1,0:T(8,128)(2,1)} fusion(bf16[1,32,16,2048]{3,2,1,0:T(8,128)(2,1)} %collective-permute-done, bf16[1,32,16,2048]{3,2,1,0:T(8,128)(2,1)} %param.5, f32[]{:T(128)} %bitcast.2, f32[]{:T(128)} %bitcast.1), kind=kLoop, calls=%fused_computation.14 | loop fusion | flops 6291456 | bytes 6291464 | tf_op jit(solution)/shard_map/convert_element_type | solution.py:25
  79.9 1.0 collective-permute-start.1
  80.9 23.4 %all-to-all-done = bf16[32,1,16,2048]{3,2,1,0:T(8,128)(2,1)S(1)} async-done(((bf16[32,1,16,2048]{3,2,1,0:T(8,128)(2,1)}), bf16[32,1,16,2048]{3,2,1,0:T(8,128)(2,1)S(1)}, u32[]{:S(2)}, u32[]{:S(2)}) %all-to-all-start) | async-done | bytes 2097184 | tf_op jit(solution)/shard_map/all_to_all | solution.py:76
  104.3 1.7 fusion
  106.7 0.4 fusion.1
  107.1 0.0 copy-start.4
  107.1 1.3 copy-done.4
  108.4 1.3 convolution_convert_fusion.4
  109.7 3.8 %add_convert_fusion.4 = bf16[512,2048]{1,0:T(8,128)(2,1)S(1)} fusion(bf16[512,2048]{1,0:T(8,128)(2,1)} %bitcast.46, bf16[512,512]{1,0:T(8,128)(2,1)S(1)} %convolution_convert_fusion.4), kind=kOutput, calls=%fused_computation.10 | convolution fusion | flops 1347682304 | bytes 4718592 | tf_op jit(solution)/shard_map/kmp,kpn->kmn/dot_general | solution.py:53
  113.5 1.3 convolution_convert_fusion.3
  114.8 2.9 %add_convert_fusion.3 = bf16[512,2048]{1,0:T(8,128)(2,1)} fusion(bf16[512,2048]{1,0:T(8,128)(2,1)S(1)} %add_convert_fusion.4, bf16[512,512]{1,0:T(8,128)(2,1)S(1)} %convolution_convert_fusion.3), kind=kOutput, calls=%fused_computation.9 | convolution fusion | flops 1347682304 | bytes 4718592 | tf_op jit(solution)/shard_map/kmp,kpn->kmn/dot_general | solution.py:53
  117.6 0.0 copy-start.6
  117.6 3.6 %convolution_convert_fusion.2 = bf16[512,512]{1,0:T(8,128)(2,1)S(1)} fusion(bf16[512,2048]{1,0:T(8,128)(2,1)} %add_convert_fusion.3), kind=kOutput, calls=%fused_computation.35 | convolution fusion | flops 1074003968 | bytes 2621440 | tf_op jit(solution)/shard_map/kmn,kpn->kmp/dot_general | solution.py:44
  121.3 0.0 copy-done.6
  121.3 2.9 %add_convert_fusion.2 = bf16[512,2048]{1,0:T(8,128)(2,1)} fusion(bf16[512,2048]{1,0:T(8,128)(2,1)S(1)} %copy-done.6, bf16[512,512]{1,0:T(8,128)(2,1)S(1)} %convolution_convert_fusion.2), kind=kOutput, calls=%fused_computation.8 | convolution fusion | flops 1347682304 | bytes 4718592 | tf_op jit(solution)/shard_map/kmp,kpn->kmn/dot_general | solution.py:53
  124.2 0.0 copy-start.7
  124.2 3.6 %convolution_convert_fusion.1 = bf16[512,512]{1,0:T(8,128)(2,1)S(1)} fusion(bf16[512,2048]{1,0:T(8,128)(2,1)} %add_convert_fusion.2), kind=kOutput, calls=%fused_computation.34 | convolution fusion | flops 1074003968 | bytes 2621440 | tf_op jit(solution)/shard_map/kmn,kpn->kmp/dot_general | solution.py:44
  127.8 0.0 copy-done.7
  127.8 2.9 %add_convert_fusion.1 = bf16[512,2048]{1,0:T(8,128)(2,1)} fusion(bf16[512,2048]{1,0:T(8,128)(2,1)S(1)} %copy-done.7, bf16[512,512]{1,0:T(8,128)(2,1)S(1)} %convolution_convert_fusion.1), kind=kOutput, calls=%fused_computation.7 | convolution fusion | flops 1347682304 | bytes 4718592 | tf_op jit(solution)/shard_map/kmp,kpn->kmn/dot_general | solution.py:53
  130.7 3.5 %convolution_convert_fusion = bf16[512,512]{1,0:T(8,128)(2,1)S(1)} fusion(bf16[512,2048]{1,0:T(8,128)(2,1)} %add_convert_fusion.1), kind=kOutput, calls=%fused_computation.33 | convolution fusion | flops 1074003968 | bytes 2621440 | tf_op jit(solution)/shard_map/kmn,kpn->kmp/dot_general | solution.py:44
  134.2 4.1 %fusion.2 = bf16[1,1,512,2048]{3,2,1,0:T(8,128)(2,1)S(1)} fusion(bf16[512,2048]{1,0:T(8,128)(2,1)} %add_convert_fusion.1, bf16[512,512]{1,0:T(8,128)(2,1)S(1)} %convolution_convert_fusion), kind=kOutput, calls=%fused_computation.15 | convolution fusion | flops 1350828032 | bytes 4718592 | tf_op jit(solution)/shard_map/kmp,kpn->kmn/dot_general | solution.py:53
  138.3 5.2 %copy.13 = bf16[1,1,512,2048]{3,1,0,2:T(2,128)(2,1)} copy(bf16[1,1,512,2048]{3,2,1,0:T(8,128)(2,1)S(1)} %fusion.2) | data formatting | bytes 4194304 | tf_op jit(solution)/shard_map/broadcast_in_dim | solution.py:61
  143.5 0.5 broadcast.97
  144.0 13.2 %reduce.2 = bf16[512,2048]{1,0:T(8,128)(2,1)S(1)} reduce(bf16[512,1,1,2048]{3,2,1,0:T(2,128)(2,1)} %bitcast.41, bf16[]{:T(256)} %broadcast.97), dimensions={1,2}, to_apply=%bitcast.40.reduce_sub_computation | reduce | bytes 4194306
  157.2 2.8 %reshape.216 = bf16[32,2,16384]{2,1,0:T(2,128)(2,1)} reshape(bf16[512,2048]{1,0:T(8,128)(2,1)S(1)} %reduce.2) | data formatting | bytes 4194304
  159.9 35.0 %all_to_all.8 = bf16[32,2,16384]{2,1,0:T(2,128)(2,1)S(1)} all-to-all(bf16[32,2,16384]{2,1,0:T(2,128)(2,1)} %reshape.216), channel_id=1, replica_groups=mesh['rep'=4,'shard'=32] {'shard'}, dimensions={0} | all-to-all | bytes 4194304 | tf_op jit(solution)/shard_map/all_to_all | solution.py:62
  195.0 6.7 %reshape.217 = bf16[512,1,1,2048]{3,2,1,0:T(2,128)(2,1)} reshape(bf16[32,2,16384]{2,1,0:T(2,128)(2,1)S(1)} %all_to_all.8) | data formatting | bytes 4194304
  201.7 3.5 %copy.11 = bf16[1,1,512,2048]{3,2,0,1:T(8,128)(2,1)S(1)} copy(bf16[1,1,512,2048]{3,1,0,2:T(2,128)(2,1)} %bitcast.42) | data formatting | bytes 4194304
  205.2 0.0 copy-start.1
  205.2 0.0 collective-permute-done.1
  205.2 5.8 %subtract_convert_fusion = bf16[1,32,16,2048]{3,2,1,0:T(8,128)(2,1)} fusion(bf16[1,32,16,2048]{3,2,1,0:T(8,128)(2,1)S(1)} %bitcast.43, bf16[1,32,16,2048]{3,2,1,0:T(8,128)(2,1)} %collective-permute-done.1, bf16[1,32,16,2048]{3,2,1,0:T(8,128)(2,1)} %add_convert_fusion.6, f32[]{:T(128)} %bitcast.3, f32[]{:T(128)} %bitcast), kind=kLoop, calls=%fused_computation.4 | loop fusion | flops 11534336 | bytes 8388616 | tf_op jit(solution)/shard_map/convert_element_type | solution.py:78
  211.0 0.0 copy-done.1
  (1 shorter events, 0.0 us)
Async XLA Ops:
  0.6 3.8 %copy-start.5 = (s32[4,2]{0,1:T(2,128)S(1)}, s32[4,2]{0,1:T(2,128)}, u32[]{:S(2)}) copy-start(s32[4,2]{0,1:T(2,128)} %param.9) | copy-start | bytes 100
  4.5 4.4 %collective-permute-start.2 = (bf16[1,32,16,2048]{3,2,1,0:T(8,128)(2,1)}, bf16[1,32,16,2048]{3,2,1,0:T(8,128)(2,1)S(1)}, u32[]{:S(2)}, u32[]{:S(2)}) collective-permute-start(bf16[1,32,16,2048]{3,2,1,0:T(8,128)(2,1)} %convert_element_type.215), channel_id=1, source_target_pairs={{0,32},{32,0},{64,96},{96,64},{1,33},{33,1},{65,97},{97,65},{2,34}... | collective-permute-start | bytes 6291464 | tf_op jit(solution)/shard_map/ppermute | solution.py:15
  8.8 51.1 %copy-start = (f32[1,32,16,2048]{3,2,1,0:T(8,128)S(1)}, f32[1,32,16,2048]{3,2,1,0:T(8,128)}, u32[]{:S(2)}) copy-start(f32[1,32,16,2048]{3,2,1,0:T(8,128)} %param.6) | copy-start | bytes 12582916
  8.8 51.1 %copy-start.2 = (bf16[1,32,16,2048]{3,2,1,0:T(8,128)(2,1)S(1)}, bf16[1,32,16,2048]{3,2,1,0:T(8,128)(2,1)}, u32[]{:S(2)}) copy-start(bf16[1,32,16,2048]{3,2,1,0:T(8,128)(2,1)} %param.8) | copy-start | bytes 6291460
  8.8 51.1 %copy-start.3 = (bf16[1,32,16,2048]{3,2,1,0:T(8,128)(2,1)S(1)}, bf16[1,32,16,2048]{3,2,1,0:T(8,128)(2,1)}, u32[]{:S(2)}) copy-start(bf16[1,32,16,2048]{3,2,1,0:T(8,128)(2,1)} %param.7) | copy-start | bytes 6291460
  11.9 48.0 %collective-permute-start.3 = (bf16[1,32,16,2048]{3,2,1,0:T(8,128)(2,1)S(1)}, bf16[1,32,16,2048]{3,2,1,0:T(8,128)(2,1)S(1)}, u32[]{:S(2)}, u32[]{:S(2)}) collective-permute-start(bf16[1,32,16,2048]{3,2,1,0:T(8,128)(2,1)S(1)} %fusion.3), channel_id=1, source_target_pairs={{0,64},{32,96},{64,0},{96,32},{1,65},{33,97},{65,1},{97,33},{2,66}... | collective-permute-start | bytes 6291464 | tf_op jit(solution)/shard_map/ppermute | solution.py:15
  14.0 61.3 %collective-permute-start = (bf16[1,32,16,2048]{3,2,1,0:T(8,128)(2,1)}, bf16[1,32,16,2048]{3,2,1,0:T(8,128)(2,1)}, u32[]{:S(2)}, u32[]{:S(2)}) collective-permute-start(bf16[1,32,16,2048]{3,2,1,0:T(8,128)(2,1)} %param.5), channel_id=1, source_target_pairs={{0,32},{32,0},{64,96},{96,64},{1,33},{33,1},{65,97},{97,65},{2,34}... | collective-permute-start | bytes 6291464 | tf_op jit(solution)/shard_map/ppermute | solution.py:15
  64.9 39.4 %all-to-all-start = ((bf16[32,1,16,2048]{3,2,1,0:T(8,128)(2,1)}), bf16[32,1,16,2048]{3,2,1,0:T(8,128)(2,1)S(1)}, u32[]{:S(2)}, u32[]{:S(2)}) async-start(bf16[32,1,16,2048]{3,2,1,0:T(8,128)(2,1)} %get-tuple-element.3), calls=%async_computation | async-start | bytes 4194304 | tf_op jit(solution)/shard_map/all_to_all | solution.py:76
  79.9 125.3 %collective-permute-start.1 = (bf16[1,32,16,2048]{3,2,1,0:T(8,128)(2,1)}, bf16[1,32,16,2048]{3,2,1,0:T(8,128)(2,1)}, u32[]{:S(2)}, u32[]{:S(2)}) collective-permute-start(bf16[1,32,16,2048]{3,2,1,0:T(8,128)(2,1)} %add_convert_fusion.6), channel_id=1, source_target_pairs={{0,64},{32,96},{64,0},{96,32},{1,65},{33,97},{65,1},{97,33},{2,66}... | collective-permute-start | bytes 6291464 | tf_op jit(solution)/shard_map/ppermute | solution.py:15
  107.1 1.3 copy-start.4
  117.6 3.7 %copy-start.6 = (bf16[512,2048]{1,0:T(8,128)(2,1)S(1)}, bf16[512,2048]{1,0:T(8,128)(2,1)}, u32[]{:S(2)}) copy-start(bf16[512,2048]{1,0:T(8,128)(2,1)} %add_convert_fusion.3) | copy-start | bytes 6291460
  124.2 3.7 %copy-start.7 = (bf16[512,2048]{1,0:T(8,128)(2,1)S(1)}, bf16[512,2048]{1,0:T(8,128)(2,1)}, u32[]{:S(2)}) copy-start(bf16[512,2048]{1,0:T(8,128)(2,1)} %add_convert_fusion.2) | copy-start | bytes 6291460
  205.2 5.8 %copy-start.1 = (bf16[1,1,512,2048]{3,2,0,1:T(8,128)(2,1)}, bf16[1,1,512,2048]{3,2,0,1:T(8,128)(2,1)S(1)}, u32[]{:S(2)}) copy-start(bf16[1,1,512,2048]{3,2,0,1:T(8,128)(2,1)S(1)} %copy.11) | copy-start | bytes 6291460
where the time goes:
time: 211 us
  waiting for transfers between devices  70.5 us (33%)
  other arithmetic  37.4 us (18%)
  blocking collectives  35 us (17%)
  matrix products  29.8 us (14%)
  local copies, waits for them, and re-layouts  20.6 us (10%)
  starting transfers between devices  13.6 us (6%)
  between operations  4.08 us (2%)
    ppermute x4, waiting for transfers between devices, swapped(): lax.ppermute(shard, axis, [(i, i ^ 1 << bit) for i in range(lax.axis_size...  47.1 us
    all_to_all x1, blocking collectives, settle(): lax.all_to_all(update_block, 'shard', split_axis=2, concat_axis=0, tiled=...  35 us
    all_to_all x1, waiting for transfers between devices, local(): lax.all_to_all(packed, 'shard', split_axis=0, concat_axis=2, tiled=True)  23.4 us
    dot_general x5, matrix products, orthogonalize(): jnp.einsum('kmp,kpn->kmn', polynomial, iterate, preferred_element_type=jn...  16.5 us
    unnamed x20, local copies, waits for them, and re-layouts  14.8 us
    dot_general x5, matrix products, orthogonalize(): jnp.einsum('kmn,kpn->kmp', iterate, iterate, preferred_element_type=jnp.f...  13.4 us
    unnamed x1, other arithmetic  13.2 us
    all_to_all x1, starting transfers between devices, local(): lax.all_to_all(packed, 'shard', split_axis=0, concat_axis=2, tiled=True)  10.5 us
  transfers between devices with their start and end apart: 5, of which 3 were waited for; matrix products, arithmetic and copies ran while one was open for 35% of the time, Pallas kernels for 0%

commit v1 on v0

--- a/solution.py
+++ b/solution.py
@@ -59,7 +59,12 @@
 
 def settle(block_in):
     update_block = orthogonalize(block_in[0])[None]
-    return lax.all_to_all(update_block, "shard", split_axis=2, concat_axis=0, tiled=True)
+    return jnp.concatenate(
+        lax.all_to_all(
+            jnp.stack(jnp.split(update_block, lax.axis_size("shard"), axis=2)), "shard", 0, 0
+        ),
+        axis=0,
+    )
 
 
 def local(weight, tracker, grad_new, grad_old, mix_keep):

time: 211 us -> 180 us (0.85)
  local copies, waits for them, and re-layouts: 20.6 us -> 3.47 us
  other arithmetic: 37.4 us -> 23.5 us
    unnamed x1 -> x0, other arithmetic: 13.2 us -> none
    unnamed x20 -> x46, local copies, waits for them, and re-layouts: 14.8 us -> 2.87 us
    broadcast_in_dim x1 -> x0, local copies, waits for them, and re-layouts: 5.18 us -> none  [settle(): update_block = orthogonalize(block_in[0])[None]]
  transfers between devices with their start and end apart: 5 -> 5, of which waited for: 3 -> 3; matrix products, arithmetic and copies ran while one was open for 35% -> 23% of each run, Pallas kernels for 0% -> 0%
where the time goes in v1:
time: 180 us
  waiting for transfers between devices  70.5 us (39%)
  blocking collectives  34.9 us (19%)
  matrix products  29.8 us (17%)
  other arithmetic  23.5 us (13%)
  starting transfers between devices  13.6 us (8%)
  between operations  4.31 us (2%)
  local copies, waits for them, and re-layouts  3.47 us (2%)
    ppermute x4, waiting for transfers between devices, swapped(): lax.ppermute(shard, axis, [(i, i ^ 1 << bit) for i in range(lax.axis_size...  47.1 us
    all_to_all x1, blocking collectives, settle(): lax.all_to_all(jnp.stack(jnp.split(update_block, lax.axis_size('shard'),...  34.9 us
    all_to_all x1, waiting for transfers between devices, local(): lax.all_to_all(packed, 'shard', split_axis=0, concat_axis=2, tiled=True)  23.4 us
    dot_general x5, matrix products, orthogonalize(): jnp.einsum('kmp,kpn->kmn', polynomial, iterate, preferred_element_type=jn...  16.5 us
    dot_general x5, matrix products, orthogonalize(): jnp.einsum('kmn,kpn->kmp', iterate, iterate, preferred_element_type=jnp.f...  13.4 us
    all_to_all x1, starting transfers between devices, local(): lax.all_to_all(packed, 'shard', split_axis=0, concat_axis=2, tiled=True)  10.5 us
    convert_element_type x2, other arithmetic, gossip_tracker(): values.astype(jnp.bfloat16)  6.91 us
    convert_element_type x1, other arithmetic, local(): (mixed_w.astype(jnp.float32) - learn_rate * update.astype(jnp.float32)).a...  5.04 us
  transfers between devices with their start and end apart: 5, of which 3 were waited for; matrix products, arithmetic and copies ran while one was open for 23% of the time, Pallas kernels for 0%

profile of v1, /device:TPU:0, one launch (start us, length us, event | category | flops | bytes accessed | tf_op | source)
XLA Modules:
  0.0 180.0 jit_solution(16182326482711121052)
XLA Ops:
  0.6 0.0 copy-start.4
  0.6 3.8 %convert_element_type.215 = bf16[1,32,16,2048]{3,2,1,0:T(8,128)(2,1)} convert(f32[1,32,16,2048]{3,2,1,0:T(8,128)} %param.6) | non-fusion elementwise | flops 1048576 | bytes 6291456 | tf_op jit(solution)/shard_map/convert_element_type | solution.py:31
  4.5 0.0 collective-permute-start.2
  4.5 0.0 copy-done.4
  4.5 0.1 constant_dynamic-slice_fusion
  4.6 0.5 fusion.34
  6.4 2.5 %collective-permute-done.2 = bf16[1,32,16,2048]{3,2,1,0:T(8,128)(2,1)S(1)} collective-permute-done((bf16[1,32,16,2048]{3,2,1,0:T(8,128)(2,1)}, bf16[1,32,16,2048]{3,2,1,0:T(8,128)(2,1)S(1)}, u32[]{:S(2)}, u32[]{:S(2)}) %collective-permute-start.2) | collective-permute-done | bytes 2097184 | tf_op jit(solution)/shard_map/ppermute | solution.py:15
  8.8 0.0 copy-start
  8.8 0.0 copy-start.1
  8.8 0.0 copy-start.2
  8.8 3.1 %fusion.3 = bf16[1,32,16,2048]{3,2,1,0:T(8,128)(2,1)S(1)} fusion(bf16[1,32,16,2048]{3,2,1,0:T(8,128)(2,1)S(1)} %collective-permute-done.2, f32[1,32,16,2048]{3,2,1,0:T(8,128)} %param.6, f32[]{:T(128)} %bitcast.2, f32[]{:T(128)} %bitcast.1), kind=kLoop, calls=%fused_computation.16 | loop fusion | flops 5242880 | bytes 8388616 | tf_op jit(solution)/shard_map/convert_element_type | solution.py:31
  11.9 2.1 %collective-permute-start.3 = (bf16[1,32,16,2048]{3,2,1,0:T(8,128)(2,1)S(1)}, bf16[1,32,16,2048]{3,2,1,0:T(8,128)(2,1)S(1)}, u32[]{:S(2)}, u32[]{:S(2)}) collective-permute-start(bf16[1,32,16,2048]{3,2,1,0:T(8,128)(2,1)S(1)} %fusion.3), channel_id=1, source_target_pairs={{0,64},{32,96},{64,0},{96,32},{1,65},{33,97},{65,1},{97,33},{2,66}... | collective-permute-start | bytes 6291464 | tf_op jit(solution)/shard_map/ppermute | solution.py:15
  14.0 0.0 collective-permute-start
  15.3 44.6 %collective-permute-done.3 = bf16[1,32,16,2048]{3,2,1,0:T(8,128)(2,1)S(1)} collective-permute-done((bf16[1,32,16,2048]{3,2,1,0:T(8,128)(2,1)S(1)}, bf16[1,32,16,2048]{3,2,1,0:T(8,128)(2,1)S(1)}, u32[]{:S(2)}, u32[]{:S(2)}) %collective-permute-start.3) | collective-permute-done | bytes 2097184 | tf_op jit(solution)/shard_map/ppermute | solution.py:15
  60.0 0.0 copy-done
  60.0 0.0 copy-done.1
  60.0 0.0 copy-done.2
  60.0 4.9 %convert_bitcast_fusion = (bf16[32,1,16,2048]{3,2,1,0:T(8,128)(2,1)}, f32[1,32,16,2048]{3,2,1,0:T(8,128)}) fusion(bf16[1,32,16,2048]{3,2,1,0:T(8,128)(2,1)S(1)} %copy-done.1, bf16[1,32,16,2048]{3,2,1,0:T(8,128)(2,1)S(1)} %copy-done.2, bf16[1,32,16,2048]{3,2,1,0:T(8,128)(2,1)S(1)} %collective-permute-done.3, f32[]{:T(128)} %bitcast.3, ...), kind=kLoop, calls=%fused_computation.17 | loop fusion | flops 13631488 | bytes 18874384 | tf_op jit(solution)/shard_map/reshape | solution.py:80
  64.9 10.5 %all-to-all-start = ((bf16[32,1,16,2048]{3,2,1,0:T(8,128)(2,1)}), bf16[32,1,16,2048]{3,2,1,0:T(8,128)(2,1)S(1)}, u32[]{:S(2)}, u32[]{:S(2)}) async-start(bf16[32,1,16,2048]{3,2,1,0:T(8,128)(2,1)} %get-tuple-element.3), calls=%async_computation | async-start | bytes 4194304 | tf_op jit(solution)/shard_map/all_to_all | solution.py:81
  75.3 0.0 collective-permute-done
  75.3 4.6 %add_convert_fusion.6 = bf16[1,32,16,2048]{3,2,1,0:T(8,128)(2,1)} fusion(bf16[1,32,16,2048]{3,2,1,0:T(8,128)(2,1)} %collective-permute-done, bf16[1,32,16,2048]{3,2,1,0:T(8,128)(2,1)} %param.5, f32[]{:T(128)} %bitcast.2, f32[]{:T(128)} %bitcast.1), kind=kLoop, calls=%fused_computation.14 | loop fusion | flops 6291456 | bytes 6291464 | tf_op jit(solution)/shard_map/convert_element_type | solution.py:25
  79.9 1.0 collective-permute-start.1
  80.9 23.4 %all-to-all-done = bf16[32,1,16,2048]{3,2,1,0:T(8,128)(2,1)S(1)} async-done(((bf16[32,1,16,2048]{3,2,1,0:T(8,128)(2,1)}), bf16[32,1,16,2048]{3,2,1,0:T(8,128)(2,1)S(1)}, u32[]{:S(2)}, u32[]{:S(2)}) %all-to-all-start) | async-done | bytes 2097184 | tf_op jit(solution)/shard_map/all_to_all | solution.py:81
  104.3 1.7 fusion
  106.7 0.4 fusion.1
  107.1 0.0 copy-start.3
  107.1 1.3 copy-done.3
  108.4 1.3 convolution_convert_fusion.4
  109.7 3.8 %add_convert_fusion.4 = bf16[512,2048]{1,0:T(8,128)(2,1)S(1)} fusion(bf16[512,2048]{1,0:T(8,128)(2,1)} %bitcast.168, bf16[512,512]{1,0:T(8,128)(2,1)S(1)} %convolution_convert_fusion.4), kind=kOutput, calls=%fused_computation.10 | convolution fusion | flops 1347682304 | bytes 4718592 | tf_op jit(solution)/shard_map/kmp,kpn->kmn/dot_general | solution.py:53
  113.5 1.3 convolution_convert_fusion.3
  114.8 2.9 %add_convert_fusion.3 = bf16[512,2048]{1,0:T(8,128)(2,1)} fusion(bf16[512,2048]{1,0:T(8,128)(2,1)S(1)} %add_convert_fusion.4, bf16[512,512]{1,0:T(8,128)(2,1)S(1)} %convolution_convert_fusion.3), kind=kOutput, calls=%fused_computation.9 | convolution fusion | flops 1347682304 | bytes 4718592 | tf_op jit(solution)/shard_map/kmp,kpn->kmn/dot_general | solution.py:53
  117.6 0.0 copy-start.5
  117.6 3.6 %convolution_convert_fusion.2 = bf16[512,512]{1,0:T(8,128)(2,1)S(1)} fusion(bf16[512,2048]{1,0:T(8,128)(2,1)} %add_convert_fusion.3), kind=kOutput, calls=%fused_computation.35 | convolution fusion | flops 1074003968 | bytes 2621440 | tf_op jit(solution)/shard_map/kmn,kpn->kmp/dot_general | solution.py:44
  121.3 0.0 copy-done.5
  121.3 2.9 %add_convert_fusion.2 = bf16[512,2048]{1,0:T(8,128)(2,1)} fusion(bf16[512,2048]{1,0:T(8,128)(2,1)S(1)} %copy-done.5, bf16[512,512]{1,0:T(8,128)(2,1)S(1)} %convolution_convert_fusion.2), kind=kOutput, calls=%fused_computation.8 | convolution fusion | flops 1347682304 | bytes 4718592 | tf_op jit(solution)/shard_map/kmp,kpn->kmn/dot_general | solution.py:53
  124.2 0.0 copy-start.6
  124.2 3.6 %convolution_convert_fusion.1 = bf16[512,512]{1,0:T(8,128)(2,1)S(1)} fusion(bf16[512,2048]{1,0:T(8,128)(2,1)} %add_convert_fusion.2), kind=kOutput, calls=%fused_computation.34 | convolution fusion | flops 1074003968 | bytes 2621440 | tf_op jit(solution)/shard_map/kmn,kpn->kmp/dot_general | solution.py:44
  127.8 0.0 copy-done.6
  127.8 2.9 %add_convert_fusion.1 = bf16[512,2048]{1,0:T(8,128)(2,1)} fusion(bf16[512,2048]{1,0:T(8,128)(2,1)S(1)} %copy-done.6, bf16[512,512]{1,0:T(8,128)(2,1)S(1)} %convolution_convert_fusion.1), kind=kOutput, calls=%fused_computation.7 | convolution fusion | flops 1347682304 | bytes 4718592 | tf_op jit(solution)/shard_map/kmp,kpn->kmn/dot_general | solution.py:53
  130.7 3.5 %convolution_convert_fusion = bf16[512,512]{1,0:T(8,128)(2,1)S(1)} fusion(bf16[512,2048]{1,0:T(8,128)(2,1)} %add_convert_fusion.1), kind=kOutput, calls=%fused_computation.33 | convolution fusion | flops 1074003968 | bytes 2621440 | tf_op jit(solution)/shard_map/kmn,kpn->kmp/dot_general | solution.py:44
  134.2 4.1 %fusion.2 = bf16[1,1,512,2048]{3,2,1,0:T(8,128)(2,1)S(1)} fusion(bf16[512,2048]{1,0:T(8,128)(2,1)} %add_convert_fusion.1, bf16[512,512]{1,0:T(8,128)(2,1)S(1)} %convolution_convert_fusion), kind=kOutput, calls=%fused_computation.15 | convolution fusion | flops 1350828032 | bytes 4718592 | tf_op jit(solution)/shard_map/kmp,kpn->kmn/dot_general | solution.py:53
  138.8 34.9 %all_to_all.14 = bf16[32,1,1,16,2048]{4,3,2,1,0:T(8,128)(2,1)S(1)} all-to-all(bf16[32,1,1,16,2048]{4,3,2,1,0:T(8,128)(2,1)S(1)} %constant_dynamic-update-slice_fusion), channel_id=1, replica_groups=mesh['rep'=4,'shard'=32] {'shard'}, dimensions={0} | all-to-all | bytes 4194304 | tf_op jit(solution)/shard_map/all_to_all | solution.py:63
  173.6 0.0 collective-permute-done.1
  173.6 5.0 %subtract_convert_fusion = bf16[1,32,16,2048]{3,2,1,0:T(8,128)(2,1)} fusion(bf16[1,32,16,2048]{3,2,1,0:T(8,128)(2,1)} %collective-permute-done.1, bf16[1,32,16,2048]{3,2,1,0:T(8,128)(2,1)} %add_convert_fusion.6, f32[]{:T(128)} %bitcast.3, f32[]{:T(128)} %bitcast, bf16[32,1,1,16,2048]{4,3,2,1,0:T(8,128)(2,1)S(1)} %all_to_all.14), kind=kLoop, calls=%fused_computation.4 | loop fusion | flops 11534336 | bytes 8388616 | tf_op jit(solution)/shard_map/convert_element_type | solution.py:83
  178.7 1.3 copy.41
  (33 shorter events, 0.2 us)
Async XLA Ops:
  0.6 3.8 %copy-start.4 = (s32[4,2]{0,1:T(2,128)S(1)}, s32[4,2]{0,1:T(2,128)}, u32[]{:S(2)}) copy-start(s32[4,2]{0,1:T(2,128)} %param.9) | copy-start | bytes 100
  4.5 4.4 %collective-permute-start.2 = (bf16[1,32,16,2048]{3,2,1,0:T(8,128)(2,1)}, bf16[1,32,16,2048]{3,2,1,0:T(8,128)(2,1)S(1)}, u32[]{:S(2)}, u32[]{:S(2)}) collective-permute-start(bf16[1,32,16,2048]{3,2,1,0:T(8,128)(2,1)} %convert_element_type.215), channel_id=1, source_target_pairs={{0,32},{32,0},{64,96},{96,64},{1,33},{33,1},{65,97},{97,65},{2,34}... | collective-permute-start | bytes 6291464 | tf_op jit(solution)/shard_map/ppermute | solution.py:15
  8.8 51.1 %copy-start = (f32[1,32,16,2048]{3,2,1,0:T(8,128)S(1)}, f32[1,32,16,2048]{3,2,1,0:T(8,128)}, u32[]{:S(2)}) copy-start(f32[1,32,16,2048]{3,2,1,0:T(8,128)} %param.6) | copy-start | bytes 12582916
  8.8 51.1 %copy-start.1 = (bf16[1,32,16,2048]{3,2,1,0:T(8,128)(2,1)S(1)}, bf16[1,32,16,2048]{3,2,1,0:T(8,128)(2,1)}, u32[]{:S(2)}) copy-start(bf16[1,32,16,2048]{3,2,1,0:T(8,128)(2,1)} %param.8) | copy-start | bytes 6291460
  8.8 51.1 %copy-start.2 = (bf16[1,32,16,2048]{3,2,1,0:T(8,128)(2,1)S(1)}, bf16[1,32,16,2048]{3,2,1,0:T(8,128)(2,1)}, u32[]{:S(2)}) copy-start(bf16[1,32,16,2048]{3,2,1,0:T(8,128)(2,1)} %param.7) | copy-start | bytes 6291460
  11.9 48.0 %collective-permute-start.3 = (bf16[1,32,16,2048]{3,2,1,0:T(8,128)(2,1)S(1)}, bf16[1,32,16,2048]{3,2,1,0:T(8,128)(2,1)S(1)}, u32[]{:S(2)}, u32[]{:S(2)}) collective-permute-start(bf16[1,32,16,2048]{3,2,1,0:T(8,128)(2,1)S(1)} %fusion.3), channel_id=1, source_target_pairs={{0,64},{32,96},{64,0},{96,32},{1,65},{33,97},{65,1},{97,33},{2,66}... | collective-permute-start | bytes 6291464 | tf_op jit(solution)/shard_map/ppermute | solution.py:15
  14.0 61.3 %collective-permute-start = (bf16[1,32,16,2048]{3,2,1,0:T(8,128)(2,1)}, bf16[1,32,16,2048]{3,2,1,0:T(8,128)(2,1)}, u32[]{:S(2)}, u32[]{:S(2)}) collective-permute-start(bf16[1,32,16,2048]{3,2,1,0:T(8,128)(2,1)} %param.5), channel_id=1, source_target_pairs={{0,32},{32,0},{64,96},{96,64},{1,33},{33,1},{65,97},{97,65},{2,34}... | collective-permute-start | bytes 6291464 | tf_op jit(solution)/shard_map/ppermute | solution.py:15
  64.9 39.4 %all-to-all-start = ((bf16[32,1,16,2048]{3,2,1,0:T(8,128)(2,1)}), bf16[32,1,16,2048]{3,2,1,0:T(8,128)(2,1)S(1)}, u32[]{:S(2)}, u32[]{:S(2)}) async-start(bf16[32,1,16,2048]{3,2,1,0:T(8,128)(2,1)} %get-tuple-element.3), calls=%async_computation | async-start | bytes 4194304 | tf_op jit(solution)/shard_map/all_to_all | solution.py:81
  79.9 93.7 %collective-permute-start.1 = (bf16[1,32,16,2048]{3,2,1,0:T(8,128)(2,1)}, bf16[1,32,16,2048]{3,2,1,0:T(8,128)(2,1)}, u32[]{:S(2)}, u32[]{:S(2)}) collective-permute-start(bf16[1,32,16,2048]{3,2,1,0:T(8,128)(2,1)} %add_convert_fusion.6), channel_id=1, source_target_pairs={{0,64},{32,96},{64,0},{96,32},{1,65},{33,97},{65,1},{97,33},{2,66}... | collective-permute-start | bytes 6291464 | tf_op jit(solution)/shard_map/ppermute | solution.py:15
  107.1 1.3 copy-start.3
  117.6 3.7 %copy-start.5 = (bf16[512,2048]{1,0:T(8,128)(2,1)S(1)}, bf16[512,2048]{1,0:T(8,128)(2,1)}, u32[]{:S(2)}) copy-start(bf16[512,2048]{1,0:T(8,128)(2,1)} %add_convert_fusion.3) | copy-start | bytes 6291460
  124.2 3.7 %copy-start.6 = (bf16[512,2048]{1,0:T(8,128)(2,1)S(1)}, bf16[512,2048]{1,0:T(8,128)(2,1)}, u32[]{:S(2)}) copy-start(bf16[512,2048]{1,0:T(8,128)(2,1)} %add_convert_fusion.2) | copy-start | bytes 6291460
